TPU v7x, 256 devices: a whole 4x4x8 slice. The times are simulated.
256 devices in a mesh: reg: 64 (over z, y, core), ep: 4 (over x).
Axes of the slice: x: 4, y: 4, z: 8, core: 2. Of those that a mesh axis runs over, the one named last changes fastest.
Arguments:
- log_prices: bfloat16 [256, 64, 256], P('reg', 'ep'), may hold values from -3 to 3
- log_wages: float32 [256, 64], P('reg', 'ep'), may hold values from -12 to 1
- labor_share: float32 [256, 256], P('reg'), may hold values from 0.3 to 0.7
- io_coeffs: bfloat16 [256, 256, 256], P('reg'), may hold values from -0.375 to 0.375
- pair_blocks: bfloat16 [256, 32, 256, 256], P('reg'), may hold values from -0.0201 to 0.801
- log_tau: float32 [256, 32, 256], P('reg'), may hold values from 0.05 to 2
- elasticity: float32 [256], replicated, may hold values from 2 to 40
- partners: int32 [256, 32], replicated, may hold values from 0 to 255, as said below
- list_lengths: int32 [256], replicated, may hold values from 1 to 32, as said below
- price_cotangent: float32 [256, 64, 256], P('reg', 'ep'), may hold values from -6 to 6
Outputs:
- new_prices: bfloat16 [256, 64, 256], P('reg', 'ep')
- price_grad: float32 [256, 64, 256], P('reg', 'ep')
- wage_grad: float32 [256, 64], P('reg', 'ep')
- tau_grad: float32 [256, 32, 256], P('reg')
Inputs may be any that keep to these rules, and one draw needn't show every extreme that they name: `partners`: each list names distinct regions. Over their live entries, the 4 importers of an aligned block name at most 2 regions of any one aligned block of 4 regions, and this is reached in every draw. `list_lengths`: in some aligned block of 4 regions every list has 32 live entries.
All inputs are finite; a program needn't handle non-finite values.
Results may differ from a plain program's by a relative error of at most 0.0064.
Values may be sent and summed in bfloat16 or wider, within the bound.
A program may use at most 64 MiB of HBM per device.

v0:
```python
import jax
import jax.numpy as jnp
from jax import lax
from jax.sharding import PartitionSpec as P


def shards(
    log_prices,
    log_wages,
    labor_share,
    io_coeffs,
    pair_blocks,
    log_tau,
    elasticity,
    partners,
    list_lengths,
    price_cotangent,
):
    own_regions, episodes, sectors = log_prices.shape
    max_slots = pair_blocks.shape[1]
    slot_total = own_regions * max_slots
    row_width = episodes * sectors
    my_index = lax.axis_index("reg")
    unit_cost = (
        labor_share[:, None, :] * log_wages[:, :, None]
        + jnp.einsum("iek,ikj->iej", log_prices, io_coeffs, preferred_element_type=jnp.float32)
    ).astype(jnp.bfloat16)
    first_region = my_index * own_regions
    my_partners = lax.dynamic_slice_in_dim(partners, first_region, own_regions, 0)
    my_lengths = lax.dynamic_slice_in_dim(list_lengths, first_region, own_regions, 0)
    slot_index = jnp.arange(max_slots, dtype=jnp.int32)
    live = slot_index[None, :] < my_lengths[:, None]
    flat_partners = my_partners.reshape(-1)
    shard_rows = lax.all_gather(unit_cost, "reg", axis=0, tiled=True)
    row_count = shard_rows.shape[0]
    selector = (flat_partners[:, None] == jnp.arange(row_count, dtype=jnp.int32)[None, :]).astype(
        jnp.bfloat16
    )
    exporter_rows = jnp.dot(
        selector, shard_rows.reshape(row_count, row_width), preferred_element_type=jnp.float32
    ).astype(jnp.bfloat16)
    exporter_rows = exporter_rows.reshape(own_regions, max_slots, episodes, sectors)
    landed = log_tau[:, :, None, :] + jnp.einsum(
        "rsek,rskj->rsej", exporter_rows, pair_blocks, preferred_element_type=jnp.float32
    )
    live_mask = live[:, :, None, None]
    scores = jnp.where(live_mask, -elasticity * landed, -jnp.inf)
    top_score = jnp.max(scores, axis=1)
    weights = jnp.exp(scores - top_score[:, None])
    total = jnp.sum(weights, axis=1)
    new_prices = (-(top_score + jnp.log(total)) / elasticity).astype(jnp.bfloat16)
    adjoint = price_cotangent[:, None] * (weights / total[:, None])
    tau_grad = lax.psum(jnp.sum(adjoint, axis=2), "ep")
    pushed = jnp.einsum(
        "rsej,rskj->rsek",
        adjoint.astype(jnp.bfloat16),
        pair_blocks,
        preferred_element_type=jnp.float32,
    ).astype(jnp.bfloat16)
    pushed = jnp.where(live_mask, pushed, jnp.zeros((), jnp.bfloat16)).reshape(
        slot_total, row_width
    )
    selector = (
        jnp.arange(own_regions * lax.axis_size("reg"), dtype=jnp.int32)[:, None]
        == flat_partners[None, :]
    ).astype(jnp.bfloat16)
    cost_adjoint = lax.psum_scatter(
        jnp.dot(selector, pushed, preferred_element_type=jnp.float32),
        "reg",
        scatter_dimension=0,
        tiled=True,
    )
    cost_adjoint = cost_adjoint.reshape(own_regions, episodes, sectors)
    price_grad = jnp.einsum(
        "iej,ikj->iek",
        cost_adjoint.astype(jnp.bfloat16),
        io_coeffs,
        preferred_element_type=jnp.float32,
    )
    wage_grad = jnp.sum(cost_adjoint * labor_share[:, None, :], axis=2)
    return (new_prices, price_grad, wage_grad, tau_grad)


def solution(mesh):
    return jax.shard_map(
        shards,
        mesh=mesh,
        in_specs=(
            P("reg", "ep", None),
            P("reg", "ep"),
            P("reg", None),
            P("reg", None, None),
            P("reg", None, None, None),
            P("reg", None, None),
            P(),
            P(),
            P(),
            P("reg", "ep", None),
        ),
        out_specs=(
            P("reg", "ep", None),
            P("reg", "ep", None),
            P("reg", "ep"),
            P("reg", None, None),
        ),
        check_vma=False,
    )
```

profile of v0, /device:TPU:8, one launch (start us, length us, event | category | flops | bytes accessed | tf_op | source)
XLA Modules:
  0.0 369.9 jit_solution(17830627746724783566)
XLA Ops:
  7.2 0.0 copy-start
  7.2 0.0 all-gather.2.cloned.1.call-start
  7.2 1.0 copy-done
  8.2 1.6 fusion.2
  9.8 0.0 all-gather.2.cloned.1.call-update
  9.8 0.0 all-reduce.6.cloned.1.call-start
  9.9 0.7 neg.6
  10.6 0.8 dynamic_slice.6
  11.3 0.8 constant_dynamic-slice_fusion.1
  12.1 0.1 copy.15
  12.2 0.1 eq.28
  12.3 0.1 iota_compare_fusion.4
  12.3 78.3 %all-gather.2.cloned.1.call-done = bf16[256,16,256]{2,1,0:T(8,128)(2,1)} async-done(((bf16[4,16,256]{2,1,0:T(8,128)(2,1)}), bf16[256,16,256]{2,1,0:T(8,128)(2,1)}) %all-gather.2.cloned.1.call-update) | async-done | bytes 2097168 | tf_op jit(solution)/shard_map/all_gather | solution.py:34
  90.6 2.5 copy.16
  93.2 0.0 copy-start.2
  93.2 0.5 convolution_convert_fusion
  93.7 0.2 copy.17
  93.9 0.1 copy-done.2
  94.1 8.1 %fusion.11 = (f32[4,16,256]{2,1,0:T(8,128)S(1)}, f32[4,32,16,256]{3,2,1,0:T(8,128)S(1)}) fusion(bf16[4,32,256,256]{3,2,1,0:T(8,128)(2,1)} %param.14, f32[4,32,256]{2,1,0:T(8,128)S(1)} %copy-done.2, f32[256]{0:T(256)S(1)} %neg.6, pred[4,32]{1,0:T(4,128)(4,1)S(1)} %iota_compare_fusion.4, bf16[4,32,16,256]{3,2,1,0:T(8,128)(2,1)S(1)} %bitcast.31), kind=kOutput, calls=%fused_computation.25 | convolution fusion | flops 270516224 | bytes 20120704 | tf_op jit(solution)/shard_map/rsek,rskj->rsej/dot_general | solution.py:43
  102.2 0.0 copy-start.1
  102.2 0.3 fusion
  102.5 0.5 copy-done.1
  103.1 11.2 %fusion.1 = bf16[4,32,16,256]{3,2,1,0:T(8,128)(2,1)} fusion(bf16[4,32,256,256]{3,2,1,0:T(8,128)(2,1)} %param.14, pred[4,32]{1,0:T(4,128)(4,1)S(1)} %iota_compare_fusion.4, f32[4,32,16,256]{3,2,1,0:T(8,128)S(1)} %get-tuple-element.5, f32[4,16,256]{2,1,0:T(8,128)S(1)} %fusion, f32[4,16,256]{2,1,0:T(8,128)S(1)} %copy-done.1, f32[4,16,256]{2,1,0:T(8,128)S(1)} %get-tuple-element.4), kind=kOutput, calls=%fused_computation.6 | convolution fusion | flops 271581184 | bytes 20119680 | tf_op jit(solution)/shard_map/rsej,rskj->rsek/dot_general | solution.py:54
  114.3 1.6 copy.18
  116.0 2.7 fusion.6
  118.6 0.0 copy-start.5
  118.6 0.0 copy-start.4
  118.6 0.0 all-reduce.6.cloned.1.call-update
  118.7 0.0 copy-start.3
  118.7 0.0 all-reduce.4.cloned.1.call-start
  118.7 0.6 copy-done.5
  119.3 0.6 dynamic-slice
  120.5 0.0 copy-done.4
  120.5 0.6 divide_convert_fusion
  121.2 1.3 fusion.5
  122.5 0.0 all-reduce.4.cloned.1.call-update
  122.5 191.0 %all-reduce.6.cloned.1.call-done = f32[256,4096]{1,0:T(8,128)} async-done(((f32[256,4096]{1,0:T(8,128)}), f32[256,4096]{1,0:T(8,128)}) %all-reduce.6.cloned.1.call-update) | async-done | bytes 4194320
  313.5 0.9 constant_dynamic-slice_fusion
  314.5 0.9 fusion.10
  315.3 0.0 copy-done.3
  315.4 0.7 fusion.7
  316.0 45.7 %all-reduce.4.cloned.1.call-done = f32[4,32,256]{2,1,0:T(8,128)} async-done(((f32[4,32,256]{2,1,0:T(8,128)}), f32[4,32,256]{2,1,0:T(8,128)}) %all-reduce.4.cloned.1.call-update) | async-done | bytes 131088 | tf_op jit(solution)/shard_map/psum | solution.py:53
  361.8 1.6 copy.25
Async XLA Ops:
  7.2 1.0 copy-start
  7.2 83.5 %all-gather.2.cloned.1.call-start = ((), (), s32[]{:S(2)}) async-start(), calls=%async_computation | async-start | bytes 2129920 | tf_op jit(solution)/shard_map/all_gather | solution.py:34
  9.8 303.7 %all-reduce.6.cloned.1.call-start = ((), (), s32[]{:S(2)}) async-start(), calls=%async_computation.2 | async-start | bytes 8388608
  93.2 0.9 copy-start.2
  102.2 0.8 copy-start.1
  118.6 0.7 copy-start.5
  118.6 1.9 copy-start.4
  118.7 196.7 %copy-start.3 = (f32[4,256]{1,0:T(4,128)S(1)}, f32[4,256]{1,0:T(4,128)}, u32[]{:S(2)}) copy-start(f32[4,256]{1,0:T(4,128)} %param.12) | copy-start | bytes 12292
  118.7 243.1 %all-reduce.4.cloned.1.call-start = ((), (), s32[]{:S(2)}) async-start(), calls=%async_computation.1 | async-start | bytes 262144 | tf_op jit(solution)/shard_map/psum | solution.py:53
Sparse Core Ops, SparseCore 0:
  11.3 79.2 all-gather.1
  118.8 194.7 all-reduce.5
  316.4 45.2 all-reduce.3
where the time goes:
time: 370 us
  waiting for transfers between devices  315 us (85%)
  matrix products  25 us (7%)
  between operations  14.5 us (4%)
  local copies, waits for them, and re-layouts  11.5 us (3%)
    unnamed x4, waiting for transfers between devices  191 us
    all_gather x1, waiting for transfers between devices, shards(): shard_rows = lax.all_gather(unit_cost, 'reg', axis=0, tiled=True)  78.3 us
    psum x1, waiting for transfers between devices, shards(): tau_grad = lax.psum(jnp.sum(adjoint, axis=2), 'ep')  45.7 us
    dot_general x1, matrix products, shards(): jnp.einsum('rsej,rskj->rsek', adjoint.astype(jnp.bfloat16), pair_blocks,...  11.2 us
    unnamed x18, local copies, waits for them, and re-layouts  9.77 us
    dot_general x1, matrix products, shards(): jnp.einsum('rsek,rskj->rsej', exporter_rows, pair_blocks, preferred_eleme...  8.14 us
  transfers between devices with their start and end apart: 3, of which 3 were waited for; matrix products, arithmetic and copies ran while one was open for 2% of the time, Pallas kernels for 0%

commit v1 on v0

--- a/solution.py
+++ b/solution.py
@@ -50,7 +50,9 @@
     total = jnp.sum(weights, axis=1)
     new_prices = (-(top_score + jnp.log(total)) / elasticity).astype(jnp.bfloat16)
     adjoint = price_cotangent[:, None] * (weights / total[:, None])
-    tau_grad = lax.psum(jnp.sum(adjoint, axis=2), "ep")
+    block = jnp.sum(adjoint, axis=2)
+    shards_2 = lax.all_gather(block, "ep", axis=0, tiled=False)
+    tau_grad = shards_2.sum(axis=0)
     pushed = jnp.einsum(
         "rsej,rskj->rsek",
         adjoint.astype(jnp.bfloat16),

time: 370 us -> 324 us (0.88)
  waiting for transfers between devices: 315 us -> 256 us
  blocking collectives: 0 us -> 13.1 us
    psum x1 -> x0, waiting for transfers between devices: 45.7 us -> none  [shards(): tau_grad = lax.psum(jnp.sum(adjoint, axis=2), 'ep')]
    unnamed x4 -> x3, waiting for transfers between devices: 191 us -> 178 us
    all_gather x0 -> x1, blocking collectives: none -> 13.1 us  [shards(): shards_2 = lax.all_gather(block, 'ep', axis=0, tiled=False)]
    unnamed x18 -> x17, local copies, waits for them, and re-layouts: 9.77 us -> 8.24 us
  transfers between devices with their start and end apart: 3 -> 2, of which waited for: 3 -> 2; matrix products, arithmetic and copies ran while one was open for 2% -> 2% of each run, Pallas kernels for 0% -> 0%
where the time goes in v1:
time: 324 us; the launch traced here: 323 us
  waiting for transfers between devices  256 us (79%)
  matrix products  25 us (8%)
  between operations  14.8 us (5%)
  blocking collectives  13.1 us (4%)
  local copies, waits for them, and re-layouts  9.94 us (3%)
  other arithmetic  3.73 us (1%)
    unnamed x3, waiting for transfers between devices  178 us
    all_gather x1, waiting for transfers between devices, shards(): shard_rows = lax.all_gather(unit_cost, 'reg', axis=0, tiled=True)  78.3 us
    all_gather x1, blocking collectives, shards(): shards_2 = lax.all_gather(block, 'ep', axis=0, tiled=False)  13.1 us
    dot_general x1, matrix products, shards(): jnp.einsum('rsej,rskj->rsek', adjoint.astype(jnp.bfloat16), pair_blocks,...  11.2 us
    unnamed x17, local copies, waits for them, and re-layouts  8.24 us
    dot_general x1, matrix products, shards(): jnp.einsum('rsek,rskj->rsej', exporter_rows, pair_blocks, preferred_eleme...  8.14 us
  transfers between devices with their start and end apart: 2, of which 2 were waited for; matrix products, arithmetic and copies ran while one was open for 2% of the time, Pallas kernels for 0%

profile of v1, /device:TPU:8, one launch (start us, length us, event | category | flops | bytes accessed | tf_op | source)
XLA Modules:
  0.0 322.9 jit_solution(4442986376792780842)
XLA Ops:
  7.2 0.0 copy-start
  7.2 0.0 all-gather.3.cloned.1.call-start
  7.2 1.0 copy-done
  8.2 1.6 fusion.2
  9.8 0.0 all-gather.3.cloned.1.call-update
  9.8 0.0 all-reduce.3.cloned.1.call-start
  9.9 0.7 neg.6
  10.6 0.8 dynamic_slice.6
  11.3 0.8 constant_dynamic-slice_fusion.1
  12.1 0.1 copy.15
  12.2 0.1 eq.28
  12.3 0.1 iota_compare_fusion.4
  12.3 78.3 %all-gather.3.cloned.1.call-done = bf16[256,16,256]{2,1,0:T(8,128)(2,1)} async-done(((bf16[4,16,256]{2,1,0:T(8,128)(2,1)}), bf16[256,16,256]{2,1,0:T(8,128)(2,1)}) %all-gather.3.cloned.1.call-update) | async-done | bytes 2097168 | tf_op jit(solution)/shard_map/all_gather | solution.py:34
  90.6 2.5 copy.16
  93.2 0.0 copy-start.2
  93.2 0.5 convolution_convert_fusion
  93.7 0.2 copy.17
  93.9 0.1 copy-done.2
  94.1 8.1 %fusion.11 = (f32[4,16,256]{2,1,0:T(8,128)S(1)}, f32[4,32,16,256]{3,2,1,0:T(8,128)S(1)}) fusion(bf16[4,32,256,256]{3,2,1,0:T(8,128)(2,1)} %param.14, f32[4,32,256]{2,1,0:T(8,128)S(1)} %copy-done.2, f32[256]{0:T(256)S(1)} %neg.6, pred[4,32]{1,0:T(4,128)(4,1)S(1)} %iota_compare_fusion.4, bf16[4,32,16,256]{3,2,1,0:T(8,128)(2,1)S(1)} %bitcast.32), kind=kOutput, calls=%fused_computation.25 | convolution fusion | flops 270516224 | bytes 20120704 | tf_op jit(solution)/shard_map/rsek,rskj->rsej/dot_general | solution.py:43
  102.2 0.0 copy-start.1
  102.2 0.3 fusion
  102.5 0.5 copy-done.1
  103.1 11.2 %fusion.1 = bf16[4,32,16,256]{3,2,1,0:T(8,128)(2,1)} fusion(bf16[4,32,256,256]{3,2,1,0:T(8,128)(2,1)} %param.14, pred[4,32]{1,0:T(4,128)(4,1)S(1)} %iota_compare_fusion.4, f32[4,32,16,256]{3,2,1,0:T(8,128)S(1)} %get-tuple-element.5, f32[4,16,256]{2,1,0:T(8,128)S(1)} %fusion, f32[4,16,256]{2,1,0:T(8,128)S(1)} %copy-done.1, f32[4,16,256]{2,1,0:T(8,128)S(1)} %get-tuple-element.4), kind=kOutput, calls=%fused_computation.6 | convolution fusion | flops 271581184 | bytes 20119680 | tf_op jit(solution)/shard_map/rsej,rskj->rsek/dot_general | solution.py:56
  114.3 1.6 copy.18
  116.0 2.7 fusion.6
  118.6 0.0 copy-start.5
  118.6 0.0 all-reduce.3.cloned.1.call-update
  118.7 0.0 copy-start.4
  118.7 0.0 copy-start.3
  118.7 0.6 copy-done.5
  119.3 0.6 dynamic-slice
  120.5 0.7 fusion.5
  121.2 13.1 %all-gather = f32[16,32,256]{2,1,0:T(8,128)S(1)} all-gather(f32[4,32,256]{2,1,0:T(8,128)S(1)} %fusion.5), channel_id=2, replica_groups=mesh['reg'=64,'ep'=4] {'ep'}, dimensions={0}, use_global_device_ids=true | all-gather | bytes 655360 | tf_op jit(solution)/shard_map/all_gather | solution.py:54
  134.3 0.7 reduce_sum.39
  135.0 0.0 copy-done.4
  135.0 0.6 divide_convert_fusion
  135.7 177.9 %all-reduce.3.cloned.1.call-done = f32[256,4096]{1,0:T(8,128)} async-done(((f32[256,4096]{1,0:T(8,128)}), f32[256,4096]{1,0:T(8,128)}) %all-reduce.3.cloned.1.call-update) | async-done | bytes 4194320
  313.5 0.9 constant_dynamic-slice_fusion
  314.5 0.0 copy-done.3
  314.5 0.7 fusion.7
  315.1 0.9 fusion.10
Async XLA Ops:
  7.2 1.0 copy-start
  7.2 83.5 %all-gather.3.cloned.1.call-start = ((), (), s32[]{:S(2)}) async-start(), calls=%async_computation | async-start | bytes 2129920 | tf_op jit(solution)/shard_map/all_gather | solution.py:34
  9.8 303.7 %all-reduce.3.cloned.1.call-start = ((), (), s32[]{:S(2)}) async-start(), calls=%async_computation.1 | async-start | bytes 8388608
  93.2 0.9 copy-start.2
  102.2 0.8 copy-start.1
  118.6 0.7 copy-start.5
  118.7 16.4 %copy-start.4 = (f32[256]{0:T(256)S(1)}, f32[256]{0:T(256)}, u32[]{:S(2)}) copy-start(f32[256]{0:T(256)} %param.16) | copy-start | bytes 3076
  118.7 195.8 %copy-start.3 = (f32[4,256]{1,0:T(4,128)S(1)}, f32[4,256]{1,0:T(4,128)}, u32[]{:S(2)}) copy-start(f32[4,256]{1,0:T(4,128)} %param.12) | copy-start | bytes 12292
Sparse Core Ops, SparseCore 0:
  11.3 79.2 all-gather.2
  118.8 194.7 all-reduce.2

commit v2 on v0

--- a/solution.py
+++ b/solution.py
@@ -1,7 +1,19 @@
+import functools
 import jax
 import jax.numpy as jnp
 from jax import lax
 from jax.sharding import PartitionSpec as P
+
+
+def page_number(s0, in_dim):
+    z_new = jnp.concatenate(
+        lax.all_to_all(jnp.stack([s0 for _ in range(lax.psum(1, "reg"))], 0), "reg", 0, 0),
+        axis=in_dim,
+    )
+    return z_new
+
+
+refer_signs = functools.partial(page_number, in_dim=0)
 
 
 def shards(
@@ -31,7 +43,7 @@
     slot_index = jnp.arange(max_slots, dtype=jnp.int32)
     live = slot_index[None, :] < my_lengths[:, None]
     flat_partners = my_partners.reshape(-1)
-    shard_rows = lax.all_gather(unit_cost, "reg", axis=0, tiled=True)
+    shard_rows = refer_signs(unit_cost)
     row_count = shard_rows.shape[0]
     selector = (flat_partners[:, None] == jnp.arange(row_count, dtype=jnp.int32)[None, :]).astype(
         jnp.bfloat16

time: 370 us -> 351 us (0.949)
  waiting for transfers between devices: 315 us -> 285 us
  starting transfers between devices: 0.12 us -> 12.3 us
    all_gather x1 -> x0, waiting for transfers between devices: 78.3 us -> none  [shards(): shard_rows = lax.all_gather(unit_cost, 'reg', axis=0, tiled=True)]
    all_to_all x0 -> x1, waiting for transfers between devices: none -> 50.8 us  [page_number(): lax.all_to_all(jnp.stack([s0 for _ in range(lax.psum(1, 'reg'))], 0), 're...]
    all_to_all x0 -> x1, starting transfers between devices: none -> 12.2 us  [page_number(): lax.all_to_all(jnp.stack([s0 for _ in range(lax.psum(1, 'reg'))], 0), 're...]
    unnamed x4 -> x3, waiting for transfers between devices: 191 us -> 189 us
    unnamed x18 -> x22, local copies, waits for them, and re-layouts: 9.77 us -> 8.23 us
where the time goes in v2:
time: 351 us; the launch traced here: 350 us
  waiting for transfers between devices  285 us (81%)
  matrix products  24.4 us (7%)
  between operations  14.8 us (4%)
  starting transfers between devices  12.3 us (4%)
  local copies, waits for them, and re-layouts  10.2 us (3%)
    unnamed x3, waiting for transfers between devices  189 us
    all_to_all x1, waiting for transfers between devices, page_number(): lax.all_to_all(jnp.stack([s0 for _ in range(lax.psum(1, 'reg'))], 0), 're...  50.8 us
    psum x1, waiting for transfers between devices, shards(): tau_grad = lax.psum(jnp.sum(adjoint, axis=2), 'ep')  45.7 us
    all_to_all x1, starting transfers between devices, page_number(): lax.all_to_all(jnp.stack([s0 for _ in range(lax.psum(1, 'reg'))], 0), 're...  12.2 us
    dot_general x1, matrix products, shards(): jnp.einsum('rsej,rskj->rsek', adjoint.astype(jnp.bfloat16), pair_blocks,...  11.2 us
    unnamed x22, local copies, waits for them, and re-layouts  8.23 us
    dot_general x1, matrix products, shards(): jnp.einsum('rsek,rskj->rsej', exporter_rows, pair_blocks, preferred_eleme...  8.14 us
  transfers between devices with their start and end apart: 3, of which 3 were waited for; matrix products, arithmetic and copies ran while one was open for 2% of the time, Pallas kernels for 0%

profile of v2, /device:TPU:8, one launch (start us, length us, event | category | flops | bytes accessed | tf_op | source)
XLA Modules:
  0.0 350.0 jit_solution(6359894717896498066)
XLA Ops:
  7.2 0.0 copy-start
  7.2 1.0 copy-done
  8.2 1.0 fusion.2
  9.2 1.6 stack.2
  10.8 0.0 copy-start.5
  10.8 0.0 copy-start.6
  10.8 0.0 copy-start.4
  10.8 12.2 %all-to-all-start = ((bf16[64,4,16,256]{3,2,1,0:T(8,128)(2,1)}), bf16[64,4,16,256]{3,2,1,0:T(8,128)(2,1)S(1)}, u32[]{:S(2)}, u32[]{:S(2)}) async-start(bf16[64,4,16,256]{3,2,1,0:T(8,128)(2,1)} %stack.2), calls=%async_computation | async-start | bytes 4194304 | tf_op jit(solution)/shard_map/all_to_all | solution.py:10
  23.0 0.0 all-reduce.6.cloned.1.call-start
  23.1 0.0 copy-done.5
  23.1 0.0 copy-done.6
  23.1 0.1 dynamic_slice.6
  23.2 0.0 copy-done.4
  23.2 0.1 constant_dynamic-slice_fusion.1
  23.3 0.1 copy.15
  23.3 0.1 eq.28
  23.4 0.1 iota_compare_fusion.4
  23.5 50.8 %all-to-all-done = bf16[64,4,16,256]{3,2,1,0:T(8,128)(2,1)S(1)} async-done(((bf16[64,4,16,256]{3,2,1,0:T(8,128)(2,1)}), bf16[64,4,16,256]{3,2,1,0:T(8,128)(2,1)S(1)}, u32[]{:S(2)}, u32[]{:S(2)}) %all-to-all-start) | async-done | bytes 2097184 | tf_op jit(solution)/shard_map/all_to_all | solution.py:10
  74.3 0.9 copy.16
  75.2 0.0 copy-start.2
  75.2 0.5 convolution_convert_fusion
  75.7 0.2 copy.17
  76.0 0.1 copy-done.2
  76.1 8.1 %fusion.11 = (f32[4,16,256]{2,1,0:T(8,128)S(1)}, f32[4,32,16,256]{3,2,1,0:T(8,128)S(1)}) fusion(bf16[4,32,256,256]{3,2,1,0:T(8,128)(2,1)} %param.14, f32[4,32,256]{2,1,0:T(8,128)S(1)} %copy-done.2, f32[256]{0:T(256)S(1)} %neg.6, pred[4,32]{1,0:T(4,128)(4,1)S(1)} %iota_compare_fusion.4, bf16[4,32,16,256]{3,2,1,0:T(8,128)(2,1)S(1)} %bitcast.33), kind=kOutput, calls=%fused_computation.25 | convolution fusion | flops 270516224 | bytes 20120704 | tf_op jit(solution)/shard_map/rsek,rskj->rsej/dot_general | solution.py:55
  84.3 0.0 copy-start.1
  84.3 0.3 fusion
  84.6 0.5 copy-done.1
  85.1 11.2 %fusion.1 = bf16[4,32,16,256]{3,2,1,0:T(8,128)(2,1)} fusion(bf16[4,32,256,256]{3,2,1,0:T(8,128)(2,1)} %param.14, pred[4,32]{1,0:T(4,128)(4,1)S(1)} %iota_compare_fusion.4, f32[4,32,16,256]{3,2,1,0:T(8,128)S(1)} %get-tuple-element.5, f32[4,16,256]{2,1,0:T(8,128)S(1)} %fusion, f32[4,16,256]{2,1,0:T(8,128)S(1)} %copy-done.1, f32[4,16,256]{2,1,0:T(8,128)S(1)} %get-tuple-element.4), kind=kOutput, calls=%fused_computation.6 | convolution fusion | flops 271581184 | bytes 20119680 | tf_op jit(solution)/shard_map/rsej,rskj->rsek/dot_general | solution.py:66
  96.3 1.6 copy.18
  98.0 2.7 fusion.6
  100.7 0.0 copy-start.7
  100.7 0.0 all-reduce.6.cloned.1.call-update
  100.7 0.0 copy-start.3
  100.7 0.0 all-reduce.4.cloned.1.call-start
  100.7 0.6 copy-done.7
  101.3 0.6 dynamic-slice
  102.6 0.6 divide_convert_fusion
  103.2 1.3 fusion.5
  104.5 0.0 all-reduce.4.cloned.1.call-update
  104.6 188.9 %all-reduce.6.cloned.1.call-done = f32[256,4096]{1,0:T(8,128)} async-done(((f32[256,4096]{1,0:T(8,128)}), f32[256,4096]{1,0:T(8,128)}) %all-reduce.6.cloned.1.call-update) | async-done | bytes 4194320
  293.4 0.9 constant_dynamic-slice_fusion
  294.3 0.9 fusion.10
  295.2 0.0 copy-done.3
  295.2 0.7 fusion.7
  295.9 45.7 %all-reduce.4.cloned.1.call-done = f32[4,32,256]{2,1,0:T(8,128)} async-done(((f32[4,32,256]{2,1,0:T(8,128)}), f32[4,32,256]{2,1,0:T(8,128)}) %all-reduce.4.cloned.1.call-update) | async-done | bytes 131088 | tf_op jit(solution)/shard_map/psum | solution.py:65
  341.6 1.6 copy.25
  (1 shorter events, 0.0 us)
Async XLA Ops:
  7.2 1.0 copy-start
  10.8 12.3 %copy-start.5 = (f32[256]{0:T(256)S(1)}, f32[256]{0:T(256)}, u32[]{:S(2)}) copy-start(f32[256]{0:T(256)} %param.16) | copy-start | bytes 3076
  10.8 12.3 %copy-start.6 = (s32[256]{0:T(256)S(1)}, s32[256]{0:T(256)}, u32[]{:S(2)}) copy-start(s32[256]{0:T(256)} %param.18) | copy-start | bytes 3076
  10.8 12.4 %copy-start.4 = (s32[256,32]{0,1:T(8,128)S(1)}, s32[256,32]{0,1:T(8,128)}, u32[]{:S(2)}) copy-start(s32[256,32]{0,1:T(8,128)} %param.17) | copy-start | bytes 98308
  10.8 63.5 %all-to-all-start = ((bf16[64,4,16,256]{3,2,1,0:T(8,128)(2,1)}), bf16[64,4,16,256]{3,2,1,0:T(8,128)(2,1)S(1)}, u32[]{:S(2)}, u32[]{:S(2)}) async-start(bf16[64,4,16,256]{3,2,1,0:T(8,128)(2,1)} %stack.2), calls=%async_computation | async-start | bytes 4194304 | tf_op jit(solution)/shard_map/all_to_all | solution.py:10
  23.0 270.4 %all-reduce.6.cloned.1.call-start = ((), (), s32[]{:S(2)}) async-start(), calls=%async_computation.2 | async-start | bytes 8388608
  75.2 0.9 copy-start.2
  84.3 0.8 copy-start.1
  100.7 0.7 copy-start.7
  100.7 194.5 %copy-start.3 = (f32[4,256]{1,0:T(4,128)S(1)}, f32[4,256]{1,0:T(4,128)}, u32[]{:S(2)}) copy-start(f32[4,256]{1,0:T(4,128)} %param.12) | copy-start | bytes 12292
  100.7 240.9 %all-reduce.4.cloned.1.call-start = ((), (), s32[]{:S(2)}) async-start(), calls=%async_computation.1 | async-start | bytes 262144 | tf_op jit(solution)/shard_map/psum | solution.py:65
Sparse Core Ops, SparseCore 0:
  100.8 192.5 all-reduce.5
  296.3 45.2 all-reduce.3
